TPU v7x, 256 devices: a whole 4x4x8 slice. The times are simulated.
256 devices in a mesh: seq: 32 (over y, x, core), grp: 8 (over z).
Axes of the slice: x: 4, y: 4, z: 8, core: 2. Of those that a mesh axis runs over, the one named last changes fastest.
Arguments:
- hidden_in: bfloat16 [98304, 2048], P(('grp', 'seq')), parts along dimension 0, may hold values from -8 to 8
- norm_gain: bfloat16 [2048], replicated, may hold values from 0.099609375 to 1.8984375
- w_query: bfloat16 [2048, 2048], P('seq'), may hold values from -1 to 1
- w_key: bfloat16 [2048, 128], P('seq'), may hold values from -1 to 1
- w_value: bfloat16 [2048, 128], P('seq'), may hold values from -0.125 to 0.125
- w_out: bfloat16 [2048, 2048], P('seq'), may hold values from -0.625 to 0.625
- seg_ids: int32 [98304], P('grp'), parts along dimension 0, may hold values from 0 to 1, never falling along the last dimension, each value on 1 to 11904 neighbouring positions
- cache_slot: int32 [768], P('grp'), parts along dimension 0, may hold values from 0 to 95, each once
Outputs:
- hidden_out: bfloat16 [98304, 2048], P(('grp', 'seq')), parts along dimension 0
- kv_cache: bfloat16 [98304, 256], P(('grp', 'seq')), parts along dimension 0
There are 8 independent parts, one for each index of `grp`. A program takes and returns all parts, laid end to end along the dimension named above; an argument that names none is the same for every part. Nothing has to cross between parts.
Inputs may be any that keep to these rules, and one draw needn't show every extreme that they name: `seg_ids`: segment numbers never fall along the stream; each prompt holds 1 to 11904 tokens. `cache_slot`: every cache position appears exactly once.
All inputs are finite; a program needn't handle non-finite values.
Results may differ from a plain program's by a relative error of at most 0.01.
Values may be sent and summed in bfloat16 or wider, within the bound.
No kernel may reach another device: no remote copies, remote signals or barrier semaphores. Data moves between devices by JAX's collectives and lax.ppermute only.
A program may use at most 256 MiB of HBM per device.

v0:
```python
import jax
import jax.numpy as jnp
from jax import lax
from jax.sharding import PartitionSpec as P

WINDOW = 1024
CACHE_BLK = 128
REACH = 3
EPSILON = 1e-06


def shifted(array, axis, by):
    length = lax.axis_size(axis)
    pairs = [(i, i + by) for i in range(length) if 0 <= i + by < length]
    return lax.ppermute(array, axis, pairs)


def normalize(hidden_in, norm_gain):
    values_wide = hidden_in.astype(jnp.float32)
    mean_square = jnp.mean(values_wide * values_wide, axis=1, keepdims=True)
    return (values_wide * lax.rsqrt(mean_square + EPSILON) * norm_gain.astype(jnp.float32)).astype(
        jnp.bfloat16
    )


def attend_block(queries, key_rows, value_rows, seg_query, seg_key, pos_query, pos_key):
    row_count = queries.shape[0]
    head_dim = key_rows.shape[1]
    head_count = queries.shape[1] // head_dim
    visible = (
        (seg_query[:, None] == seg_key[None, :])
        & (pos_key[None, :] <= pos_query[:, None])
        & (pos_key[None, :] > pos_query[:, None] - WINDOW)
    )
    score_scale = 1.0 / head_dim**0.5

    def one_head(query_head):
        scores = (
            lax.dot_general(
                query_head, key_rows, (((1,), (1,)), ((), ())), preferred_element_type=jnp.float32
            )
            * score_scale
        )
        scores = jnp.where(visible, scores, -jnp.inf)
        row_top = jnp.max(scores, axis=1, keepdims=True)
        weights = jnp.exp(scores - row_top).astype(jnp.bfloat16)
        weight_sum = jnp.sum(weights.astype(jnp.float32), axis=1, keepdims=True)
        mixture = jnp.dot(weights, value_rows, preferred_element_type=jnp.float32) / weight_sum
        return mixture.astype(jnp.bfloat16)

    per_head = jnp.transpose(queries.reshape(row_count, head_count, head_dim), (1, 0, 2))
    result = lax.map(one_head, per_head)
    return jnp.transpose(result, (1, 0, 2)).reshape(row_count, head_count * head_dim)


def shards(hidden_in, norm_gain, w_query, w_key, w_value, w_out, seg_ids, cache_slot):
    row_count = hidden_in.shape[0]
    devices = lax.axis_size("seq")
    my_index = lax.axis_index("seq")
    normed = normalize(hidden_in, norm_gain)
    head_dim = w_key.shape[1]
    pieces = (
        lax.all_gather(w_query, "seq", axis=0, tiled=True),
        lax.all_gather(w_key, "seq", axis=0, tiled=True),
        lax.all_gather(w_value, "seq", axis=0, tiled=True),
    )
    columns = normed
    query_sum, key_sum, value_sum = tuple(
        (jnp.dot(columns, piece, preferred_element_type=jnp.float32) for piece in pieces)
    )
    query = query_sum.astype(jnp.bfloat16)
    stacked = jnp.concatenate(
        [key_sum.astype(jnp.bfloat16), value_sum.astype(jnp.bfloat16)], axis=1
    )
    margin = REACH * row_count
    span = (REACH + 1) * row_count
    reach_now = min(REACH, devices - 1)
    missing = jnp.zeros(((REACH - reach_now) * row_count, 2 * head_dim), jnp.bfloat16)
    received = []
    current = stacked
    for distance in range(reach_now):
        current = shifted(current, "seq", 1)
        received.append(current)
    window_rows = jnp.concatenate([missing] + received[::-1] + [stacked], axis=0)
    first_row = my_index * row_count
    seg_pad = jnp.concatenate([jnp.full((margin,), -1, jnp.int32), seg_ids])
    seg_query = lax.dynamic_slice_in_dim(seg_ids, first_row, row_count, 0)
    seg_key = lax.dynamic_slice_in_dim(seg_pad, first_row, span, 0)
    pos_query = first_row + jnp.arange(row_count, dtype=jnp.int32)
    pos_key = first_row - margin + jnp.arange(span, dtype=jnp.int32)
    attended = attend_block(
        query,
        window_rows[:, :head_dim],
        window_rows[:, head_dim:],
        seg_query,
        seg_key,
        pos_query,
        pos_key,
    )
    columns = attended
    projected = jnp.dot(
        columns,
        lax.all_gather(w_out, "seq", axis=0, tiled=True),
        preferred_element_type=jnp.float32,
    )
    hidden_out = (hidden_in.astype(jnp.float32) + projected).astype(jnp.bfloat16)
    blocks_per_dev = row_count // CACHE_BLK
    block_total = cache_slot.shape[0]
    slot_ids = jnp.arange(block_total, dtype=jnp.int32)
    source_of = jnp.sum(
        jnp.where(cache_slot[None, :] == slot_ids[:, None], slot_ids[None, :], 0), axis=1
    )
    owned_sources = lax.dynamic_slice_in_dim(
        source_of, my_index * blocks_per_dev, blocks_per_dev, 0
    )
    within = jnp.arange(row_count, dtype=jnp.int32)
    source_row = (
        jnp.repeat(owned_sources, CACHE_BLK, total_repeat_length=row_count) * CACHE_BLK
        + within % CACHE_BLK
    )
    piece = lax.all_gather(stacked, "seq", axis=0, tiled=True)
    inside = (source_row >= 0) & (source_row < piece.shape[0])
    taken = jnp.take(piece, jnp.clip(source_row, 0, piece.shape[0] - 1), axis=0)
    kv_cache = jnp.where(inside[:, None], taken, jnp.zeros_like(stacked))
    return (hidden_out, kv_cache)


def solution(mesh):
    in_specs = (
        P(("grp", "seq"), None),
        P(),
        P("seq", None),
        P("seq", None),
        P("seq", None),
        P("seq", None),
        P("grp"),
        P("grp"),
    )
    out_specs = (P(("grp", "seq"), None), P(("grp", "seq"), None))
    return jax.shard_map(shards, mesh=mesh, in_specs=in_specs, out_specs=out_specs, check_vma=False)
```

profile of v0, /device:TPU:1, one launch (start us, length us, event | category | flops | bytes accessed | tf_op | source)
XLA Modules:
  0.0 271.4 jit_solution(2322478954140555485)
XLA Ops:
  9.8 26.4 %all_gather.17 = bf16[2048,128]{1,0:T(8,128)(2,1)S(1)} all-gather(bf16[64,128]{1,0:T(8,128)(2,1)} %param.16), channel_id=1, replica_groups=mesh['seq'=32,'grp'=8] {'seq'}, dimensions={0}, use_global_device_ids=true | all-gather | bytes 540672 | tf_op jit(solution)/shard_map/all_gather | solution.py:65
  36.3 24.1 %all_gather.16 = bf16[2048,128]{1,0:T(8,128)(2,1)S(1)} all-gather(bf16[64,128]{1,0:T(8,128)(2,1)} %param.15), channel_id=1, replica_groups=mesh['seq'=32,'grp'=8] {'seq'}, dimensions={0}, use_global_device_ids=true | all-gather | bytes 540672 | tf_op jit(solution)/shard_map/all_gather | solution.py:64
  63.4 1.9 collective-permute-start
  66.3 2.0 fusion.23
  68.4 4.1 %collective-permute-start.1 = (bf16[384,256]{0,1:T(8,128)(2,1)S(1)}, bf16[384,256]{0,1:T(8,128)(2,1)S(1)}, u32[]{:S(2)}, u32[]{:S(2)}) collective-permute-start(bf16[384,256]{0,1:T(8,128)(2,1)S(1)} %collective-permute-done), channel_id=1, source_target_pairs={{0,8},{8,16},{16,24},{24,32},{32,40},{40,48},{48,56},{56,64},{64,7... | collective-permute-start | bytes 589832 | tf_op jit(solution)/shard_map/ppermute | solution.py:15
  72.5 2.6 collective-permute-done.1
  75.1 4.6 %collective-permute-start.2 = (bf16[384,256]{0,1:T(8,128)(2,1)S(1)}, bf16[384,256]{0,1:T(8,128)(2,1)S(1)}, u32[]{:S(2)}, u32[]{:S(2)}) collective-permute-start(bf16[384,256]{0,1:T(8,128)(2,1)S(1)} %collective-permute-done.1), channel_id=1, source_target_pairs={{0,8},{8,16},{16,24},{24,32},{32,40},{40,48},{48,56},{56,64},{64,7... | collective-permute-start | bytes 589832 | tf_op jit(solution)/shard_map/ppermute | solution.py:15
  79.7 3.3 %collective-permute-done.2 = bf16[384,256]{0,1:T(8,128)(2,1)S(1)} collective-permute-done((bf16[384,256]{0,1:T(8,128)(2,1)S(1)}, bf16[384,256]{0,1:T(8,128)(2,1)S(1)}, u32[]{:S(2)}, u32[]{:S(2)}) %collective-permute-start.2) | collective-permute-done | bytes 196640 | tf_op jit(solution)/shard_map/ppermute | solution.py:15
  84.9 37.7 %all-gather.8.cloned.1.call-done = bf16[12288,256]{0,1:T(8,128)(2,1)} async-done(((bf16[384,256]{0,1:T(8,128)(2,1)}), bf16[12288,256]{0,1:T(8,128)(2,1)}) %all-gather.8.cloned.1.call-update) | async-done | bytes 6291472 | tf_op jit(solution)/shard_map/all_gather | solution.py:121
  122.7 8.6 %copy.23 = bf16[12288,256]{1,0:T(8,128)(2,1)} copy(bf16[12288,256]{0,1:T(8,128)(2,1)} %all-gather.8.cloned.1.call-done) | data formatting | bytes 12582912 | tf_op jit(solution)/shard_map/all_gather | solution.py:121
  131.3 5.3 %gather_fusion = bf16[384,256]{1,0:T(8,128)(2,1)S(1)} fusion(bf16[12288,256]{1,0:T(8,128)(2,1)} %copy.23, s32[1024]{0:T(1024)S(1)} %pad_clamp_fusion), kind=kCustom, calls=%fused_computation | custom fusion | bytes 394752 | tf_op jit(solution)/shard_map/jit(_take)/gather | solution.py:123
  137.4 45.4 %all-gather.4.cloned.1.call-done = bf16[2048,2048]{1,0:T(8,128)(2,1)} async-done(((bf16[64,2048]{1,0:T(8,128)(2,1)}), bf16[2048,2048]{1,0:T(8,128)(2,1)}) %all-gather.4.cloned.1.call-update) | async-done | bytes 8388624 | tf_op jit(solution)/shard_map/all_gather | solution.py:63
  182.8 6.8 %fusion.12 = bf16[48,16,8,128]{3,2,1,0:T(8,128)(2,1)S(1)} fusion(bf16[2048,2048]{1,0:T(8,128)(2,1)} %all-gather.4.cloned.1.call-done, bf16[384,2048]{1,0:T(8,128)(2,1)S(1)} %copy-done, f32[2048]{0:T(1024)S(1)} %convert_element_type.32, f32[384]{0:T(512)S(1)} %add_rsqrt_fusion), kind=kOutput, calls=%fused_computation.22 | convolution fusion | flops 3225157632 | bytes 11544064 | tf_op jit(solution)/shard_map/dot_general | solution.py:69
  190.1 66.2 %while.12 = (s32[]{:T(128)}, bf16[16,384,128]{1,2,0:T(8,128)(2,1)}, bf16[16,384,128]{2,1,0:T(8,128)(2,1)S(1)}, bf16[1536,128]{1,0:T(8,128)(2,1)}, bf16[1536,128]...) while((s32[]{:T(128)}, bf16[16,384,128]{1,2,0:T(8,128)(2,1)}, ...), condition=%wide.region_4.5_spmd.clone, body=%wide.region_1.4_spmd.clone.sunk | while | flops 309165312 | bytes 10055833 | solution.py:52
  194.2 1.9 fusion.47
  206.6 1.9 fusion.47
  214.9 1.9 fusion.47
  219.0 1.9 fusion.47
  223.2 1.9 fusion.47
  227.3 1.9 fusion.47
  231.5 1.9 fusion.47
  235.6 1.9 fusion.47
  239.8 1.9 fusion.47
  256.3 8.5 %fusion.11 = bf16[384,2048]{1,0:T(8,128)(2,1)} fusion(bf16[384,2048]{1,0:T(8,128)(2,1)S(1)} %copy-done, bf16[384,2048]{0,1:T(8,128)(2,1)} %bitcast.62, bf16[2048,2048]{1,0:T(8,128)(2,1)} %all-gather.6.cloned.1.call-done), kind=kOutput, calls=%fused_computation.19 | convolution fusion | flops 3223584768 | bytes 13107200 | tf_op jit(solution)/shard_map/dot_general | solution.py:101
  (140 shorter events, 58.9 us)
Async XLA Ops:
  7.2 53.2 %copy-start = (bf16[384,2048]{1,0:T(8,128)(2,1)S(1)}, bf16[384,2048]{1,0:T(8,128)(2,1)}, u32[]{:S(2)}) copy-start(bf16[384,2048]{1,0:T(8,128)(2,1)} %param.12) | copy-start | bytes 4718596
  7.2 115.5 %all-gather.8.cloned.1.call-start = ((), (), s32[]{:S(2)}) async-start(), calls=%async_computation.2 | async-start | bytes 6488064 | tf_op jit(solution)/shard_map/all_gather | solution.py:121
  61.1 4.3 %copy-start.3 = (s32[96]{0:T(128)S(1)}, s32[96]{0:T(128)}, u32[]{:S(2)}) copy-start(s32[96]{0:T(128)} %param.19) | copy-start | bytes 1156
  61.1 5.1 %copy-start.2 = (s32[12288]{0:T(1024)S(1)}, s32[12288]{0:T(1024)}, u32[]{:S(2)}) copy-start(s32[12288]{0:T(1024)} %param.18) | copy-start | bytes 147460
  62.6 120.3 %all-gather.4.cloned.1.call-start = ((), (), s32[]{:S(2)}) async-start(), calls=%async_computation | async-start | bytes 8650752 | tf_op jit(solution)/shard_map/all_gather | solution.py:63
  63.3 193.0 %all-gather.6.cloned.1.call-start = ((), (), s32[]{:S(2)}) async-start(), calls=%async_computation.1 | async-start | bytes 8650752 | tf_op jit(solution)/shard_map/all_gather | solution.py:103
  63.4 5.0 %collective-permute-start = (bf16[384,256]{0,1:T(8,128)(2,1)}, bf16[384,256]{0,1:T(8,128)(2,1)S(1)}, u32[]{:S(2)}, u32[]{:S(2)}) collective-permute-start(bf16[384,256]{0,1:T(8,128)(2,1)} %pad_maximum_fusion), channel_id=1, source_target_pairs={{0,8},{8,16},{16,24},{24,32},{32,40},{40,48},{48,56},{56,64},{64,7... | collective-permute-start | bytes 589832 | tf_op jit(solution)/shard_map/ppermute | solution.py:15
  68.4 6.7 %collective-permute-start.1 = (bf16[384,256]{0,1:T(8,128)(2,1)S(1)}, bf16[384,256]{0,1:T(8,128)(2,1)S(1)}, u32[]{:S(2)}, u32[]{:S(2)}) collective-permute-start(bf16[384,256]{0,1:T(8,128)(2,1)S(1)} %collective-permute-done), channel_id=1, source_target_pairs={{0,8},{8,16},{16,24},{24,32},{32,40},{40,48},{48,56},{56,64},{64,7... | collective-permute-start | bytes 589832 | tf_op jit(solution)/shard_map/ppermute | solution.py:15
  75.1 7.9 %collective-permute-start.2 = (bf16[384,256]{0,1:T(8,128)(2,1)S(1)}, bf16[384,256]{0,1:T(8,128)(2,1)S(1)}, u32[]{:S(2)}, u32[]{:S(2)}) collective-permute-start(bf16[384,256]{0,1:T(8,128)(2,1)S(1)} %collective-permute-done.1), channel_id=1, source_target_pairs={{0,8},{8,16},{16,24},{24,32},{32,40},{40,48},{48,56},{56,64},{64,7... | collective-permute-start | bytes 589832 | tf_op jit(solution)/shard_map/ppermute | solution.py:15
  192.0 1.0 copy-start.1
  196.1 1.0 copy-start.1
  200.2 1.0 copy-start.1
  204.4 1.0 copy-start.1
  212.6 1.0 copy-start.1
  216.7 1.0 copy-start.1
  220.9 1.0 copy-start.1
  225.1 1.0 copy-start.1
  229.2 1.0 copy-start.1
  233.4 1.0 copy-start.1
  237.5 1.0 copy-start.1
  241.7 1.0 copy-start.1
  245.8 1.0 copy-start.1
  249.9 1.0 copy-start.1
  254.1 1.0 copy-start.1
  (1 other events, 1.0 us)
Sparse Core Ops, SparseCore 0:
  62.7 59.9 all-gather.7
  125.2 57.5 all-gather.3
  185.4 57.5 all-gather.5
where the time goes:
time: 273 us; the launch traced here: 271 us
  waiting for transfers between devices  89.7 us (33%)
  matrix products  54.3 us (20%)
  blocking collectives  50.5 us (18%)
  local copies, waits for them, and re-layouts  37.7 us (14%)
  other arithmetic  14.3 us (5%)
  between operations  13.9 us (5%)
  starting transfers between devices  10.7 us (4%)
    all_gather x1, waiting for transfers between devices, shards(): lax.all_gather(w_query, 'seq', axis=0, tiled=True)  45.4 us
    all_gather x1, waiting for transfers between devices, shards(): piece = lax.all_gather(stacked, 'seq', axis=0, tiled=True)  37.7 us
    dot_general x16, matrix products, one_head(): lax.dot_general(query_head, key_rows, (((1,), (1,)), ((), ())), preferred...  30 us
    all_gather x1, blocking collectives, shards(): lax.all_gather(w_value, 'seq', axis=0, tiled=True)  26.4 us
    all_gather x1, blocking collectives, shards(): lax.all_gather(w_key, 'seq', axis=0, tiled=True)  24.1 us
    dynamic_update_slice x32, local copies, waits for them, and re-layouts, attend_block(): result = lax.map(one_head, per_head)  12.5 us
    ppermute x3, starting transfers between devices, shifted(): return lax.ppermute(array, axis, pairs)  10.5 us
    all_gather x1, local copies, waits for them, and re-layouts, shards(): piece = lax.all_gather(stacked, 'seq', axis=0, tiled=True)  8.63 us
  transfers between devices with their start and end apart: 6, of which 4 were waited for; matrix products, arithmetic and copies ran while one was open for 31% of the time, Pallas kernels for 0%

commit v1 on v0

--- a/solution.py
+++ b/solution.py
@@ -54,6 +54,15 @@
 
 
 def shards(hidden_in, norm_gain, w_query, w_key, w_value, w_out, seg_ids, cache_slot):
+
+    def take_meshes(raw):
+        return jnp.concatenate(
+            lax.all_to_all(
+                jnp.stack([raw for _ in range(lax.axis_size("seq"))], axis=0), "seq", 0, 0
+            ),
+            axis=0,
+        )
+
     row_count = hidden_in.shape[0]
     devices = lax.axis_size("seq")
     my_index = lax.axis_index("seq")
@@ -62,7 +71,7 @@
     pieces = (
         lax.all_gather(w_query, "seq", axis=0, tiled=True),
         lax.all_gather(w_key, "seq", axis=0, tiled=True),
-        lax.all_gather(w_value, "seq", axis=0, tiled=True),
+        take_meshes(w_value),
     )
     columns = normed
     query_sum, key_sum, value_sum = tuple(

time: 273 us -> 258 us (0.945)
  blocking collectives: 50.5 us -> 27.6 us
  starting transfers between devices: 10.7 us -> 19.5 us
    all_gather x1 -> x0, blocking collectives: 26.4 us -> none  [shards(): lax.all_gather(w_value, 'seq', axis=0, tiled=True)]
    all_to_all x0 -> x1, starting transfers between devices: none -> 8.59 us  [take_meshes(): lax.all_to_all(jnp.stack([raw for _ in range(lax.axis_size('seq'))], axis...]
    all_gather x1, waiting for transfers between devices: 37.7 us -> 33.3 us  [shards(): piece = lax.all_gather(stacked, 'seq', axis=0, tiled=True)]
    ppermute x3, waiting for transfers between devices: 5.86 us -> 9.39 us  [shifted(): return lax.ppermute(array, axis, pairs)]
    all_gather x1, blocking collectives: 24.1 us -> 27.6 us  [shards(): lax.all_gather(w_key, 'seq', axis=0, tiled=True)]
  transfers between devices with their start and end apart: 6 -> 7, of which waited for: 4 -> 5; matrix products, arithmetic and copies ran while one was open for 31% -> 33% of each run, Pallas kernels for 0% -> 0%
where the time goes in v1:
time: 258 us; the launch traced here: 256 us
  waiting for transfers between devices  89.5 us (35%)
  matrix products  54.3 us (21%)
  local copies, waits for them, and re-layouts  39.3 us (15%)
  blocking collectives  27.6 us (11%)
  starting transfers between devices  19.5 us (8%)
  between operations  14 us (5%)
  other arithmetic  11.9 us (5%)
    all_gather x1, waiting for transfers between devices, shards(): lax.all_gather(w_query, 'seq', axis=0, tiled=True)  45.4 us
    all_gather x1, waiting for transfers between devices, shards(): piece = lax.all_gather(stacked, 'seq', axis=0, tiled=True)  33.3 us
    dot_general x16, matrix products, one_head(): lax.dot_general(query_head, key_rows, (((1,), (1,)), ((), ())), preferred...  30 us
    all_gather x1, blocking collectives, shards(): lax.all_gather(w_key, 'seq', axis=0, tiled=True)  27.6 us
    dynamic_update_slice x32, local copies, waits for them, and re-layouts, attend_block(): result = lax.map(one_head, per_head)  12.5 us
    ppermute x3, starting transfers between devices, shifted(): return lax.ppermute(array, axis, pairs)  10.7 us
    ppermute x3, waiting for transfers between devices, shifted(): return lax.ppermute(array, axis, pairs)  9.39 us
    all_gather x1, local copies, waits for them, and re-layouts, shards(): piece = lax.all_gather(stacked, 'seq', axis=0, tiled=True)  8.62 us
  transfers between devices with their start and end apart: 7, of which 5 were waited for; matrix products, arithmetic and copies ran while one was open for 33% of the time, Pallas kernels for 0%

profile of v1, /device:TPU:1, one launch (start us, length us, event | category | flops | bytes accessed | tf_op | source)
XLA Modules:
  0.0 256.3 jit_solution(11627310281379975193)
XLA Ops:
  8.9 8.6 %all-to-all-start = ((bf16[32,64,128]{2,1,0:T(8,128)(2,1)}), bf16[32,64,128]{2,1,0:T(8,128)(2,1)S(1)}, u32[]{:S(2)}, u32[]{:S(2)}) async-start(bf16[32,64,128]{2,1,0:T(8,128)(2,1)} %stack.2), calls=%async_computation | async-start | bytes 1048576 | tf_op jit(solution)/shard_map/all_to_all | solution.py:60
  18.0 27.6 %all_gather.13 = bf16[2048,128]{1,0:T(8,128)(2,1)S(1)} all-gather(bf16[64,128]{1,0:T(8,128)(2,1)S(1)} %copy-done.3), channel_id=1, replica_groups=mesh['seq'=32,'grp'=8] {'seq'}, dimensions={0}, use_global_device_ids=true | all-gather | bytes 540672 | tf_op jit(solution)/shard_map/all_gather | solution.py:73
  52.1 1.9 collective-permute-start
  54.1 2.8 %collective-permute-done = bf16[384,256]{0,1:T(8,128)(2,1)S(1)} collective-permute-done((bf16[384,256]{0,1:T(8,128)(2,1)}, bf16[384,256]{0,1:T(8,128)(2,1)S(1)}, u32[]{:S(2)}, u32[]{:S(2)}) %collective-permute-start) | collective-permute-done | bytes 196640 | tf_op jit(solution)/shard_map/ppermute | solution.py:15
  56.9 4.3 %collective-permute-start.1 = (bf16[384,256]{0,1:T(8,128)(2,1)S(1)}, bf16[384,256]{0,1:T(8,128)(2,1)S(1)}, u32[]{:S(2)}, u32[]{:S(2)}) collective-permute-start(bf16[384,256]{0,1:T(8,128)(2,1)S(1)} %collective-permute-done), channel_id=1, source_target_pairs={{0,8},{8,16},{16,24},{24,32},{32,40},{40,48},{48,56},{56,64},{64,7... | collective-permute-start | bytes 589832 | tf_op jit(solution)/shard_map/ppermute | solution.py:15
  61.2 3.1 %collective-permute-done.1 = bf16[384,256]{0,1:T(8,128)(2,1)S(1)} collective-permute-done((bf16[384,256]{0,1:T(8,128)(2,1)S(1)}, bf16[384,256]{0,1:T(8,128)(2,1)S(1)}, u32[]{:S(2)}, u32[]{:S(2)}) %collective-permute-start.1) | collective-permute-done | bytes 196640 | tf_op jit(solution)/shard_map/ppermute | solution.py:15
  64.3 4.6 %collective-permute-start.2 = (bf16[384,256]{0,1:T(8,128)(2,1)S(1)}, bf16[384,256]{0,1:T(8,128)(2,1)S(1)}, u32[]{:S(2)}, u32[]{:S(2)}) collective-permute-start(bf16[384,256]{0,1:T(8,128)(2,1)S(1)} %collective-permute-done.1), channel_id=1, source_target_pairs={{0,8},{8,16},{16,24},{24,32},{32,40},{40,48},{48,56},{56,64},{64,7... | collective-permute-start | bytes 589832 | tf_op jit(solution)/shard_map/ppermute | solution.py:15
  68.9 3.5 %collective-permute-done.2 = bf16[384,256]{0,1:T(8,128)(2,1)S(1)} collective-permute-done((bf16[384,256]{0,1:T(8,128)(2,1)S(1)}, bf16[384,256]{0,1:T(8,128)(2,1)S(1)}, u32[]{:S(2)}, u32[]{:S(2)}) %collective-permute-start.2) | collective-permute-done | bytes 196640 | tf_op jit(solution)/shard_map/ppermute | solution.py:15
  74.4 33.3 %all-gather.8.cloned.1.call-done = bf16[12288,256]{0,1:T(8,128)(2,1)} async-done(((bf16[384,256]{0,1:T(8,128)(2,1)}), bf16[12288,256]{0,1:T(8,128)(2,1)}) %all-gather.8.cloned.1.call-update) | async-done | bytes 6291472 | tf_op jit(solution)/shard_map/all_gather | solution.py:130
  107.7 8.6 %copy.23 = bf16[12288,256]{1,0:T(8,128)(2,1)} copy(bf16[12288,256]{0,1:T(8,128)(2,1)} %all-gather.8.cloned.1.call-done) | data formatting | bytes 12582912 | tf_op jit(solution)/shard_map/all_gather | solution.py:130
  116.3 5.3 %gather_fusion = bf16[384,256]{1,0:T(8,128)(2,1)S(1)} fusion(bf16[12288,256]{1,0:T(8,128)(2,1)} %copy.23, s32[1024]{0:T(1024)S(1)} %pad_clamp_fusion), kind=kCustom, calls=%fused_computation | custom fusion | bytes 394752 | tf_op jit(solution)/shard_map/jit(_take)/gather | solution.py:132
  122.4 45.4 %all-gather.4.cloned.1.call-done = bf16[2048,2048]{1,0:T(8,128)(2,1)} async-done(((bf16[64,2048]{1,0:T(8,128)(2,1)}), bf16[2048,2048]{1,0:T(8,128)(2,1)}) %all-gather.4.cloned.1.call-update) | async-done | bytes 8388624 | tf_op jit(solution)/shard_map/all_gather | solution.py:72
  167.8 6.8 %fusion.12 = bf16[48,16,8,128]{3,2,1,0:T(8,128)(2,1)S(1)} fusion(bf16[2048,2048]{1,0:T(8,128)(2,1)} %all-gather.4.cloned.1.call-done, bf16[384,2048]{1,0:T(8,128)(2,1)S(1)} %copy-done, f32[2048]{0:T(1024)S(1)} %convert_element_type.32, f32[384]{0:T(512)S(1)} %add_rsqrt_fusion), kind=kOutput, calls=%fused_computation.22 | convolution fusion | flops 3225157632 | bytes 11544064 | tf_op jit(solution)/shard_map/dot_general | solution.py:78
  175.1 66.2 %while.12 = (s32[]{:T(128)}, bf16[16,384,128]{1,2,0:T(8,128)(2,1)}, bf16[16,384,128]{2,1,0:T(8,128)(2,1)S(1)}, bf16[1536,128]{1,0:T(8,128)(2,1)}, bf16[1536,128]...) while((s32[]{:T(128)}, bf16[16,384,128]{1,2,0:T(8,128)(2,1)}, ...), condition=%wide.region_4.5_spmd.clone, body=%wide.region_1.4_spmd.clone.sunk | while | flops 309165312 | bytes 10055833 | solution.py:52
  175.1 1.9 fusion.47
  179.2 1.9 fusion.47
  191.6 1.9 fusion.47
  195.8 1.9 fusion.47
  208.2 1.9 fusion.47
  212.3 1.9 fusion.47
  216.4 1.9 fusion.47
  220.6 1.9 fusion.47
  224.8 1.9 fusion.47
  241.3 8.5 %fusion.11 = bf16[384,2048]{1,0:T(8,128)(2,1)} fusion(bf16[384,2048]{1,0:T(8,128)(2,1)S(1)} %copy-done, bf16[384,2048]{0,1:T(8,128)(2,1)} %bitcast.64, bf16[2048,2048]{1,0:T(8,128)(2,1)} %all-gather.6.cloned.1.call-done), kind=kOutput, calls=%fused_computation.19 | convolution fusion | flops 3223584768 | bytes 13107200 | tf_op jit(solution)/shard_map/dot_general | solution.py:110
  (146 shorter events, 60.9 us)
Async XLA Ops:
  7.2 10.4 %copy-start = (bf16[384,2048]{1,0:T(8,128)(2,1)S(1)}, bf16[384,2048]{1,0:T(8,128)(2,1)}, u32[]{:S(2)}) copy-start(bf16[384,2048]{1,0:T(8,128)(2,1)} %param.12) | copy-start | bytes 4718596
  7.2 10.8 %copy-start.3 = (bf16[64,128]{1,0:T(8,128)(2,1)S(1)}, bf16[64,128]{1,0:T(8,128)(2,1)}, u32[]{:S(2)}) copy-start(bf16[64,128]{1,0:T(8,128)(2,1)} %param.15) | copy-start | bytes 49156
  7.2 38.4 %copy-start.4 = (bf16[2048]{0:T(1024)(128)(2,1)S(1)}, bf16[2048]{0:T(1024)(128)(2,1)}, u32[]{:S(2)}) copy-start(bf16[2048]{0:T(1024)(128)(2,1)} %param.13) | copy-start | bytes 12292
  8.9 37.4 %all-to-all-start = ((bf16[32,64,128]{2,1,0:T(8,128)(2,1)}), bf16[32,64,128]{2,1,0:T(8,128)(2,1)S(1)}, u32[]{:S(2)}, u32[]{:S(2)}) async-start(bf16[32,64,128]{2,1,0:T(8,128)(2,1)} %stack.2), calls=%async_computation | async-start | bytes 1048576 | tf_op jit(solution)/shard_map/all_to_all | solution.py:60
  17.5 90.1 %all-gather.8.cloned.1.call-start = ((), (), s32[]{:S(2)}) async-start(), calls=%async_computation.3 | async-start | bytes 6488064 | tf_op jit(solution)/shard_map/all_gather | solution.py:130
  46.4 3.0 %copy-start.5 = (s32[96]{0:T(128)S(1)}, s32[96]{0:T(128)}, u32[]{:S(2)}) copy-start(s32[96]{0:T(128)} %param.19) | copy-start | bytes 1156
  46.4 3.8 %copy-start.2 = (s32[12288]{0:T(1024)S(1)}, s32[12288]{0:T(1024)}, u32[]{:S(2)}) copy-start(s32[12288]{0:T(1024)} %param.18) | copy-start | bytes 147460
  47.8 120.0 %all-gather.4.cloned.1.call-start = ((), (), s32[]{:S(2)}) async-start(), calls=%async_computation.1 | async-start | bytes 8650752 | tf_op jit(solution)/shard_map/all_gather | solution.py:72
  48.6 192.7 %all-gather.6.cloned.1.call-start = ((), (), s32[]{:S(2)}) async-start(), calls=%async_computation.2 | async-start | bytes 8650752 | tf_op jit(solution)/shard_map/all_gather | solution.py:112
  52.1 4.8 %collective-permute-start = (bf16[384,256]{0,1:T(8,128)(2,1)}, bf16[384,256]{0,1:T(8,128)(2,1)S(1)}, u32[]{:S(2)}, u32[]{:S(2)}) collective-permute-start(bf16[384,256]{0,1:T(8,128)(2,1)} %pad_maximum_fusion), channel_id=1, source_target_pairs={{0,8},{8,16},{16,24},{24,32},{32,40},{40,48},{48,56},{56,64},{64,7... | collective-permute-start | bytes 589832 | tf_op jit(solution)/shard_map/ppermute | solution.py:15
  56.9 7.4 %collective-permute-start.1 = (bf16[384,256]{0,1:T(8,128)(2,1)S(1)}, bf16[384,256]{0,1:T(8,128)(2,1)S(1)}, u32[]{:S(2)}, u32[]{:S(2)}) collective-permute-start(bf16[384,256]{0,1:T(8,128)(2,1)S(1)} %collective-permute-done), channel_id=1, source_target_pairs={{0,8},{8,16},{16,24},{24,32},{32,40},{40,48},{48,56},{56,64},{64,7... | collective-permute-start | bytes 589832 | tf_op jit(solution)/shard_map/ppermute | solution.py:15
  64.3 8.1 %collective-permute-start.2 = (bf16[384,256]{0,1:T(8,128)(2,1)S(1)}, bf16[384,256]{0,1:T(8,128)(2,1)S(1)}, u32[]{:S(2)}, u32[]{:S(2)}) collective-permute-start(bf16[384,256]{0,1:T(8,128)(2,1)S(1)} %collective-permute-done.1), channel_id=1, source_target_pairs={{0,8},{8,16},{16,24},{24,32},{32,40},{40,48},{48,56},{56,64},{64,7... | collective-permute-start | bytes 589832 | tf_op jit(solution)/shard_map/ppermute | solution.py:15
  177.0 1.0 copy-start.1
  181.1 1.0 copy-start.1
  189.4 1.0 copy-start.1
  197.6 1.0 copy-start.1
  201.7 1.0 copy-start.1
  205.9 1.0 copy-start.1
  210.0 1.0 copy-start.1
  214.2 1.0 copy-start.1
  218.3 1.0 copy-start.1
  222.5 1.0 copy-start.1
  230.8 1.0 copy-start.1
  234.9 1.0 copy-start.1
  (4 other events, 4.0 us)
Sparse Core Ops, SparseCore 0:
  48.0 59.6 all-gather.7
  110.2 57.5 all-gather.3
  170.4 57.5 all-gather.5
